TPU v7x, 32 devices: a whole 2x2x4 slice. The times are simulated.
32 devices in a mesh: dp: 4 (over z), mp: 8 (over y, x, core).
Axes of the slice: x: 2, y: 2, z: 4, core: 2. Of those that a mesh axis runs over, the one named last changes fastest.
Arguments:
- behaviors: bfloat16 [32, 2048, 1024], P('dp', 'mp'), may hold values from -8 to 8
- candidates: bfloat16 [32, 2048, 128], P('dp', 'mp'), may hold values from -12 to 12
- lengths: int32 [32], P('dp'), may hold values from 128 to 1024
- bilinear: bfloat16 [2048, 2048], P('mp'), may hold values from -1 to 2
- norm_gain: float32 [2048], replicated, may hold values from 0.1 to 1.9
- w_gate: bfloat16 [2048, 8192], P('dp', 'mp'), may hold values from -0.125 to 0.125
- w_up: bfloat16 [2048, 8192], P('dp', 'mp'), may hold values from -0.125 to 0.125
- w_down: bfloat16 [8192, 2048], P('mp', 'dp'), may hold values from -0.0625 to 0.0625
Outputs:
- interest: bfloat16 [32, 2048, 128], P('dp', 'mp')
All inputs are finite; a program needn't handle non-finite values.
Results may differ from a plain program's by a relative error of at most 0.015.
Values may be sent and summed in bfloat16 or wider, within the bound.
No kernel may reach another device: no remote copies, remote signals or barrier semaphores. Data moves between devices by JAX's collectives and lax.ppermute only.
A program may use at most 64 MiB of HBM per device.

v0:
```python
import math
import jax
import jax.numpy as jnp
from jax import lax
from jax.sharding import PartitionSpec as P


def attention_weights(scores, live):
    masked = jnp.where(live, scores, -1e30)
    highest = jnp.max(masked, axis=-1, keepdims=True)
    expons = jnp.where(live, jnp.exp(masked - highest), 0.0)
    return (expons / jnp.sum(expons, axis=-1, keepdims=True)).astype(jnp.bfloat16)


def shards(behaviors, candidates, lengths, bilinear, norm_gain, w_gate, w_up, w_down):
    user_count, width_part, cand_count = candidates.shape
    feature_width = bilinear.shape[1]
    behavior_count = behaviors.shape[2]
    query_part = jnp.einsum(
        "ek,ukc->uec",
        bilinear,
        lax.all_gather(candidates, "mp", axis=1, tiled=True),
        preferred_element_type=jnp.float32,
    )
    query = query_part.astype(jnp.bfloat16)
    partial_value = jnp.einsum("ukc,ukl->ucl", query, behaviors, preferred_element_type=jnp.float32)
    scale = 1.0 / math.sqrt(feature_width)
    live = (
        lax.broadcasted_iota(jnp.int32, (user_count, 1, behavior_count), 2) < lengths[:, None, None]
    )
    share = lax.psum_scatter(partial_value, "mp", scatter_dimension=1, tiled=True)
    probs_share = attention_weights(share * scale, live)
    probs = lax.all_gather(probs_share, "mp", axis=1, tiled=True)
    pooled = jnp.einsum(
        "ucl,ukl->ukc", probs, behaviors, preferred_element_type=jnp.float32
    ).astype(jnp.bfloat16)
    whole = lax.all_gather(pooled, "mp", axis=1, tiled=True)
    values = whole.astype(jnp.float32)
    square_mean = jnp.mean(values * values, axis=1, keepdims=True)
    normed = (values * lax.rsqrt(square_mean + 1e-06) * norm_gain[None, :, None]).astype(
        jnp.bfloat16
    )
    gate = jnp.einsum(
        "ukc,kf->ucf",
        normed,
        lax.all_gather(w_gate, "dp", axis=0, tiled=True),
        preferred_element_type=jnp.float32,
    )
    upward = jnp.einsum(
        "ukc,kf->ucf",
        normed,
        lax.all_gather(w_up, "dp", axis=0, tiled=True),
        preferred_element_type=jnp.float32,
    )
    hidden = (jax.nn.silu(gate) * upward).astype(jnp.bfloat16)
    down_full = lax.all_gather(w_down, "dp", axis=1, tiled=True)
    result = lax.psum_scatter(
        jnp.einsum("ucf,fk->kuc", hidden, down_full, preferred_element_type=jnp.float32).astype(
            jnp.bfloat16
        ),
        "mp",
        scatter_dimension=0,
        tiled=True,
    ).astype(jnp.float32)
    return jnp.transpose(result, (1, 0, 2)).astype(jnp.bfloat16)


def solution(mesh):
    return jax.shard_map(
        shards,
        mesh=mesh,
        in_specs=(
            P("dp", "mp", None),
            P("dp", "mp", None),
            P("dp"),
            P("mp", None),
            P(),
            P("dp", "mp"),
            P("dp", "mp"),
            P("mp", "dp"),
        ),
        out_specs=P("dp", "mp", None),
        check_vma=False,
    )
```

profile of v0, /device:TPU:0, one launch (start us, length us, event | category | flops | bytes accessed | tf_op | source)
XLA Modules:
  0.0 498.7 jit_solution(1023455317639719504)
XLA Ops:
  6.5 0.0 copy-start
  6.5 0.0 all-gather.7.cloned.1.call-start
  6.5 0.7 all-gather.7.cloned.1.call-update
  7.3 0.0 reduce-scatter.3.cloned.1.call-start
  7.3 41.3 %all-gather.7.cloned.1.call-done = bf16[8,2048,128]{2,1,0:T(8,128)(2,1)} async-done(((bf16[8,256,128]{2,1,0:T(8,128)(2,1)}), bf16[8,2048,128]{2,1,0:T(8,128)(2,1)}) %all-gather.7.cloned.1.call-update) | async-done | bytes 4194320 | tf_op jit(solution)/shard_map/all_gather | solution.py:22
  48.6 0.0 copy-done
  48.6 8.2 %fusion.24 = f32[8,128,1024]{2,1,0:T(8,128)} fusion(bf16[8,256,1024]{2,1,0:T(8,128)(2,1)} %param.8, bf16[8,2048,128]{2,1,0:T(8,128)(2,1)} %all-gather.7.cloned.1.call-done, bf16[256,2048]{1,0:T(8,128)(2,1)S(1)} %copy-done), kind=kOutput, calls=%fused_computation.18 | convolution fusion | flops 1610874880 | bytes 13631488 | tf_op jit(solution)/shard_map/ukc,ukl->ucl/dot_general | solution.py:26
  56.7 0.0 copy-start.1
  56.7 0.0 reduce-scatter.3.cloned.1.call-update
  56.8 0.0 all-gather.9.cloned.1.call-start
  56.8 0.6 copy-done.1
  57.4 0.1 iota_compare_fusion
  57.5 50.5 %reduce-scatter.3.cloned.1.call-done = f32[8,16,1024]{2,1,0:T(8,128)} async-done(((f32[8,128,1024]{2,1,0:T(8,128)}), f32[8,16,1024]{2,1,0:T(8,128)}) %reduce-scatter.3.cloned.1.call-update) | async-done | bytes 524304 | tf_op jit(solution)/shard_map/reduce_scatter | solution.py:31
  108.0 1.7 fusion.37
  109.7 0.8 divide_convert_fusion
  110.5 0.0 all-gather.9.cloned.1.call-update
  110.6 0.0 all-gather.11.cloned.1.call-start
  110.6 27.9 %all-gather.9.cloned.1.call-done = bf16[8,128,1024]{2,1,0:T(8,128)(2,1)} async-done(((bf16[8,16,1024]{2,1,0:T(8,128)(2,1)}), bf16[8,128,1024]{2,1,0:T(8,128)(2,1)}) %all-gather.9.cloned.1.call-update) | async-done | bytes 2097168 | tf_op jit(solution)/shard_map/all_gather | solution.py:33
  138.5 5.2 %fusion.27 = bf16[8,256,128]{1,2,0:T(8,128)(2,1)} fusion(bf16[8,128,1024]{2,1,0:T(8,128)(2,1)} %all-gather.9.cloned.1.call-done, bf16[8,256,1024]{2,1,0:T(8,128)(2,1)} %param.8), kind=kOutput, calls=%fused_computation.21 | convolution fusion | flops 537133056 | bytes 6815744 | tf_op jit(solution)/shard_map/ucl,ukl->ukc/dot_general | solution.py:34
  143.7 0.0 copy-start.2
  143.7 0.0 all-gather.11.cloned.1.call-update
  143.7 0.0 all-gather.13.cloned.1.call-start
  143.7 0.5 all-gather.13.cloned.1.call-update
  144.3 0.0 all-gather.15.cloned.1.call-start
  144.3 0.5 all-gather.15.cloned.1.call-update
  144.8 0.0 all-gather.17.cloned.1.call-start
  144.9 0.7 all-gather.17.cloned.1.call-update
  145.6 0.2 reduce-scatter.5.cloned.1.call-start
  145.8 35.4 %all-gather.11.cloned.1.call-done = bf16[8,2048,128]{1,2,0:T(8,128)(2,1)} async-done(((bf16[8,256,128]{1,2,0:T(8,128)(2,1)}), bf16[8,2048,128]{1,2,0:T(8,128)(2,1)}) %all-gather.11.cloned.1.call-update) | async-done | bytes 4194320 | tf_op jit(solution)/shard_map/all_gather | solution.py:37
  181.2 3.1 fusion.1
  184.3 79.1 %all-gather.13.cloned.1.call-done = bf16[2048,1024]{1,0:T(8,128)(2,1)} async-done(((bf16[512,1024]{1,0:T(8,128)(2,1)}), bf16[2048,1024]{1,0:T(8,128)(2,1)}) %all-gather.13.cloned.1.call-update) | async-done | bytes 4194320 | tf_op jit(solution)/shard_map/all_gather | solution.py:46
  263.4 0.0 copy-done.2
  263.4 9.9 %fusion.8 = f32[8,128,1024]{2,1,0:T(8,128)} fusion(bf16[2048,1024]{1,0:T(8,128)(2,1)} %all-gather.13.cloned.1.call-done, bf16[8,2048,128]{1,2,0:T(8,128)(2,1)} %all-gather.11.cloned.1.call-done, f32[2048]{0:T(1024)S(1)} %copy-done.2, f32[8,128]{1,0:T(8,128)S(1)} %add_rsqrt_fusion), kind=kOutput, calls=%fused_computation.10 | convolution fusion | flops 4303355904 | bytes 12595200 | tf_op jit(solution)/shard_map/ukc,kf->ucf/dot_general | solution.py:43
  273.3 70.7 %all-gather.15.cloned.1.call-done = bf16[2048,1024]{1,0:T(8,128)(2,1)} async-done(((bf16[512,1024]{1,0:T(8,128)(2,1)}), bf16[2048,1024]{1,0:T(8,128)(2,1)}) %all-gather.15.cloned.1.call-update) | async-done | bytes 4194320 | tf_op jit(solution)/shard_map/all_gather | solution.py:52
  344.0 80.8 %all-gather.17.cloned.1.call-done = bf16[1024,2048]{1,0:T(8,128)(2,1)} async-done(((bf16[1024,512]{1,0:T(8,128)(2,1)}), bf16[1024,2048]{1,0:T(8,128)(2,1)}) %all-gather.17.cloned.1.call-update) | async-done | bytes 4194320 | tf_op jit(solution)/shard_map/all_gather | solution.py:56
  424.9 15.2 %convert_bitcast_fusion = bf16[2048,8,128]{0,2,1:T(8,128)(2,1)} fusion(bf16[1024,2048]{1,0:T(8,128)(2,1)} %all-gather.17.cloned.1.call-done, f32[8,128,1024]{2,1,0:T(8,128)} %fusion.8, bf16[2048,1024]{1,0:T(8,128)(2,1)} %all-gather.15.cloned.1.call-done, bf16[8,2048,128]{1,2,0:T(8,128)(2,1)} %all-gather.11.cloned.1.call-done, f32[2048]{0:T(1024)S(1)} %copy-done.2, ...), kind=kOutput, calls=%fused_computation.12 | convolution fusion | flops 8606711808 | bytes 20983808 | tf_op jit(solution)/shard_map/ucf,fk->kuc/dot_general | solution.py:58
  440.1 0.0 reduce-scatter.5.cloned.1.call-update
  440.1 49.7 %reduce-scatter.5.cloned.1.call-done = bf16[256,8,128]{0,2,1:T(8,128)(2,1)} async-done(((bf16[2048,8,128]{0,2,1:T(8,128)(2,1)}), bf16[256,8,128]{0,2,1:T(8,128)(2,1)}) %reduce-scatter.5.cloned.1.call-update) | async-done | bytes 524304 | tf_op jit(solution)/shard_map/reduce_scatter | solution.py:57
  489.8 2.0 copy.9
  (1 shorter events, 0.0 us)
Async XLA Ops:
  6.5 42.0 %copy-start = (bf16[256,2048]{1,0:T(8,128)(2,1)S(1)}, bf16[256,2048]{1,0:T(8,128)(2,1)}, u32[]{:S(2)}) copy-start(bf16[256,2048]{1,0:T(8,128)(2,1)} %param.11) | copy-start | bytes 3145732
  6.5 42.0 %all-gather.7.cloned.1.call-start = ((), (), s32[]{:S(2)}) async-start(), calls=%async_computation.2 | async-start | bytes 4718592 | tf_op jit(solution)/shard_map/all_gather | solution.py:22
  7.3 100.8 %reduce-scatter.3.cloned.1.call-start = ((), (), s32[]{:S(2)}) async-start(), calls=%async_computation.3 | async-start | bytes 4718592 | tf_op jit(solution)/shard_map/reduce_scatter | solution.py:31
  56.7 0.7 copy-start.1
  56.8 81.7 %all-gather.9.cloned.1.call-start = ((), (), s32[]{:S(2)}) async-start(), calls=%async_computation.4 | async-start | bytes 2359296 | tf_op jit(solution)/shard_map/all_gather | solution.py:33
  110.6 70.6 %all-gather.11.cloned.1.call-start = ((), (), s32[]{:S(2)}) async-start(), calls=%async_computation.5 | async-start | bytes 4718592 | tf_op jit(solution)/shard_map/all_gather | solution.py:37
  143.7 119.7 %copy-start.2 = (f32[2048]{0:T(1024)S(1)}, f32[2048]{0:T(1024)}, u32[]{:S(2)}) copy-start(f32[2048]{0:T(1024)} %param.12) | copy-start | bytes 24580
  143.7 119.7 %all-gather.13.cloned.1.call-start = ((), (), s32[]{:S(2)}) async-start(), calls=%async_computation.6 | async-start | bytes 5242880 | tf_op jit(solution)/shard_map/all_gather | solution.py:46
  144.3 199.8 %all-gather.15.cloned.1.call-start = ((), (), s32[]{:S(2)}) async-start(), calls=%async_computation.7 | async-start | bytes 5242880 | tf_op jit(solution)/shard_map/all_gather | solution.py:52
  144.8 280.0 %all-gather.17.cloned.1.call-start = ((), (), s32[]{:S(2)}) async-start(), calls=%async_computation.8 | async-start | bytes 5242880 | tf_op jit(solution)/shard_map/all_gather | solution.py:56
  145.6 344.2 %reduce-scatter.5.cloned.1.call-start = ((), (), s32[]{:S(2)}) async-start(), calls=%async_computation.9 | async-start | bytes 4718592 | tf_op jit(solution)/shard_map/reduce_scatter | solution.py:57
Sparse Core Ops, SparseCore 0:
  9.2 39.2 all-gather.6
  56.9 51.0 reduce-scatter.2
  110.7 27.7 all-gather.8
  143.8 37.3 all-gather.10
  182.6 80.7 all-gather.12
  264.8 79.2 all-gather.14
  345.6 79.2 all-gather.16
  440.2 49.5 reduce-scatter.4
where the time goes:
time: 499 us
  waiting for transfers between devices  438 us (88%)
  matrix products  38.4 us (8%)
  between operations  13.5 us (3%)
  other arithmetic  5.68 us (1%)
    all_gather x1, waiting for transfers between devices, shards(): down_full = lax.all_gather(w_down, 'dp', axis=1, tiled=True)  80.8 us
    all_gather x1, waiting for transfers between devices, shards(): lax.all_gather(w_gate, 'dp', axis=0, tiled=True)  79.1 us
    all_gather x1, waiting for transfers between devices, shards(): lax.all_gather(w_up, 'dp', axis=0, tiled=True)  70.7 us
    reduce_scatter x1, waiting for transfers between devices, shards(): lax.psum_scatter(partial_value, 'mp', scatter_dimension=1, tiled=True)  50.5 us
    reduce_scatter x1, waiting for transfers between devices, shards(): lax.psum_scatter(jnp.einsum('ucf,fk->kuc', hidden, down_full, preferred_e...  49.7 us
    all_gather x1, waiting for transfers between devices, shards(): lax.all_gather(candidates, 'mp', axis=1, tiled=True)  41.3 us
    all_gather x1, waiting for transfers between devices, shards(): whole = lax.all_gather(pooled, 'mp', axis=1, tiled=True)  35.4 us
    all_gather x1, waiting for transfers between devices, shards(): probs = lax.all_gather(probs_share, 'mp', axis=1, tiled=True)  27.9 us
  transfers between devices with their start and end apart: 8, of which 8 were waited for; matrix products, arithmetic and copies ran while one was open for 3% of the time, Pallas kernels for 0%

commit v1 on v0

--- a/solution.py
+++ b/solution.py
@@ -53,7 +53,21 @@
         preferred_element_type=jnp.float32,
     )
     hidden = (jax.nn.silu(gate) * upward).astype(jnp.bfloat16)
-    down_full = lax.all_gather(w_down, "dp", axis=1, tiled=True)
+
+    def _match_cube(chunk):
+        which_axis = "dp"
+        axis_n = jax.lax.axis_size(which_axis)
+        arr_out = [(i - 1, i) for i in range(1, axis_n)] + [(axis_n - 1, 0)]
+        top = chunk
+        slots = [top]
+        for _ in tuple(range(axis_n - 1)):
+            top = jax.lax.ppermute(top, which_axis, arr_out)
+            slots += [top]
+        clean = jnp.concatenate([*reversed(slots)], 1)
+        wide_out = jnp.roll(clean, (jax.lax.axis_index(which_axis) + 1) * top.shape[1], 1)
+        return wide_out
+
+    down_full = _match_cube(w_down)
     result = lax.psum_scatter(
         jnp.einsum("ucf,fk->kuc", hidden, down_full, preferred_element_type=jnp.float32).astype(
             jnp.bfloat16

time: 499 us -> 442 us (0.89)
  waiting for transfers between devices: 438 us -> 367 us
  local copies, waits for them, and re-layouts: 2.63 us -> 14.5 us
    ppermute x0 -> x3, waiting for transfers between devices: none -> 106 us  [_match_cube(): top = jax.lax.ppermute(top, which_axis, arr_out)]
    all_gather x1 -> x0, waiting for transfers between devices: 80.8 us -> none  [shards(): down_full = lax.all_gather(w_down, 'dp', axis=1, tiled=True)]
    all_gather x1, waiting for transfers between devices: 70.7 us -> 20 us  [shards(): lax.all_gather(w_up, 'dp', axis=0, tiled=True)]
    all_gather x1, waiting for transfers between devices: 35.4 us -> 0.01 us  [shards(): whole = lax.all_gather(pooled, 'mp', axis=1, tiled=True)]
    unnamed x6 -> x16, local copies, waits for them, and re-layouts: 0.59 us -> 13.5 us
    all_gather x1, waiting for transfers between devices: 79.1 us -> 69.5 us  [shards(): lax.all_gather(w_gate, 'dp', axis=0, tiled=True)]
  transfers between devices with their start and end apart: 8 -> 10, of which waited for: 8 -> 9; matrix products, arithmetic and copies ran while one was open for 3% -> 6% of each run, Pallas kernels for 0% -> 0%
where the time goes in v1:
time: 442 us; the launch traced here: 441 us
  waiting for transfers between devices  367 us (83%)
  matrix products  39.1 us (9%)
  local copies, waits for them, and re-layouts  14.5 us (3%)
  between operations  13.5 us (3%)
  other arithmetic  5.65 us (1%)
    ppermute x3, waiting for transfers between devices, _match_cube(): top = jax.lax.ppermute(top, which_axis, arr_out)  106 us
    all_gather x1, waiting for transfers between devices, shards(): lax.all_gather(w_gate, 'dp', axis=0, tiled=True)  69.5 us
    reduce_scatter x1, waiting for transfers between devices, shards(): lax.psum_scatter(partial_value, 'mp', scatter_dimension=1, tiled=True)  50.5 us
    reduce_scatter x1, waiting for transfers between devices, shards(): lax.psum_scatter(jnp.einsum('ucf,fk->kuc', hidden, down_full, preferred_e...  49.7 us
    all_gather x1, waiting for transfers between devices, shards(): lax.all_gather(candidates, 'mp', axis=1, tiled=True)  41.3 us
    all_gather x1, waiting for transfers between devices, shards(): probs = lax.all_gather(probs_share, 'mp', axis=1, tiled=True)  27.9 us
    all_gather x1, waiting for transfers between devices, shards(): lax.all_gather(w_up, 'dp', axis=0, tiled=True)  20 us
    dot_general x1, matrix products, shards(): jnp.einsum('ucf,fk->kuc', hidden, down_full, preferred_element_type=jnp.f...  15.8 us
  transfers between devices with their start and end apart: 10, of which 9 were waited for; matrix products, arithmetic and copies ran while one was open for 6% of the time, Pallas kernels for 0%

profile of v1, /device:TPU:0, one launch (start us, length us, event | category | flops | bytes accessed | tf_op | source)
XLA Modules:
  0.0 441.2 jit_solution(1074521576066140140)
XLA Ops:
  6.5 0.0 copy-start
  6.5 0.0 all-gather.6.cloned.1.call-start
  6.5 0.7 all-gather.6.cloned.1.call-update
  7.3 0.0 reduce-scatter.3.cloned.1.call-start
  7.3 41.3 %all-gather.6.cloned.1.call-done = bf16[8,2048,128]{2,1,0:T(8,128)(2,1)} async-done(((bf16[8,256,128]{2,1,0:T(8,128)(2,1)}), bf16[8,2048,128]{2,1,0:T(8,128)(2,1)}) %all-gather.6.cloned.1.call-update) | async-done | bytes 4194320 | tf_op jit(solution)/shard_map/all_gather | solution.py:22
  48.6 0.0 copy-done
  48.6 8.2 %fusion.18 = f32[8,128,1024]{2,1,0:T(8,128)} fusion(bf16[8,256,1024]{2,1,0:T(8,128)(2,1)} %param.8, bf16[8,2048,128]{2,1,0:T(8,128)(2,1)} %all-gather.6.cloned.1.call-done, bf16[256,2048]{1,0:T(8,128)(2,1)S(1)} %copy-done), kind=kOutput, calls=%fused_computation.19 | convolution fusion | flops 1610874880 | bytes 13631488 | tf_op jit(solution)/shard_map/ukc,ukl->ucl/dot_general | solution.py:26
  56.7 0.0 copy-start.2
  56.8 0.0 reduce-scatter.3.cloned.1.call-update
  56.8 0.0 all-gather.8.cloned.1.call-start
  56.8 0.6 copy-done.2
  57.4 0.1 iota_compare_fusion
  57.5 50.5 %reduce-scatter.3.cloned.1.call-done = f32[8,16,1024]{2,1,0:T(8,128)} async-done(((f32[8,128,1024]{2,1,0:T(8,128)}), f32[8,16,1024]{2,1,0:T(8,128)}) %reduce-scatter.3.cloned.1.call-update) | async-done | bytes 524304 | tf_op jit(solution)/shard_map/reduce_scatter | solution.py:31
  108.0 1.6 fusion.40
  109.7 0.8 divide_convert_fusion
  110.5 0.0 all-gather.8.cloned.1.call-update
  110.5 0.0 copy-start.1
  110.5 0.0 all-gather.10.cloned.1.call-start
  110.6 27.9 %all-gather.8.cloned.1.call-done = bf16[8,128,1024]{2,1,0:T(8,128)(2,1)} async-done(((bf16[8,16,1024]{2,1,0:T(8,128)(2,1)}), bf16[8,128,1024]{2,1,0:T(8,128)(2,1)}) %all-gather.8.cloned.1.call-update) | async-done | bytes 2097168 | tf_op jit(solution)/shard_map/all_gather | solution.py:33
  138.4 5.1 %fusion.21 = bf16[8,256,128]{1,2,0:T(8,128)(2,1)} fusion(bf16[8,128,1024]{2,1,0:T(8,128)(2,1)} %all-gather.8.cloned.1.call-done, bf16[8,256,1024]{2,1,0:T(8,128)(2,1)} %param.8), kind=kOutput, calls=%fused_computation.22 | convolution fusion | flops 537133056 | bytes 6815744 | tf_op jit(solution)/shard_map/ucl,ukl->ukc/dot_general | solution.py:34
  143.6 0.0 all-gather.10.cloned.1.call-update
  143.6 0.0 all-gather.14.cloned.1.call-start
  143.7 0.5 all-gather.14.cloned.1.call-update
  144.2 0.0 all-gather.12.cloned.1.call-start
  144.3 0.5 all-gather.12.cloned.1.call-update
  144.8 0.0 reduce-scatter.5.cloned.1.call-start
  144.8 0.0 copy-done.1
  144.8 0.5 copy.9
  145.4 1.5 collective-permute-start
  146.9 25.6 %collective-permute-done = bf16[1024,512]{0,1:T(8,128)(2,1)S(1)} collective-permute-done((bf16[1024,512]{0,1:T(8,128)(2,1)S(1)}, bf16[1024,512]{0,1:T(8,128)(2,1)S(1)}, u32[]{:S(2)}, u32[]{:S(2)}) %collective-permute-start) | collective-permute-done | bytes 1048608 | tf_op jit(solution)/shard_map/ppermute | solution.py:64
  172.5 0.0 collective-permute-start.1
  172.5 31.4 %collective-permute-done.1 = bf16[1024,512]{0,1:T(8,128)(2,1)} collective-permute-done((bf16[1024,512]{0,1:T(8,128)(2,1)S(1)}, bf16[1024,512]{0,1:T(8,128)(2,1)}, u32[]{:S(2)}, u32[]{:S(2)}) %collective-permute-start.1) | collective-permute-done | bytes 1048608 | tf_op jit(solution)/shard_map/ppermute | solution.py:64
  203.9 0.0 collective-permute-start.2
  203.9 48.8 %collective-permute-done.2 = bf16[1024,512]{0,1:T(8,128)(2,1)} collective-permute-done((bf16[1024,512]{0,1:T(8,128)(2,1)}, bf16[1024,512]{0,1:T(8,128)(2,1)}, u32[]{:S(2)}, u32[]{:S(2)}) %collective-permute-start.2) | collective-permute-done | bytes 1048608 | tf_op jit(solution)/shard_map/ppermute | solution.py:64
  252.7 2.3 constant_dynamic-update-slice_fusion.7
  255.0 2.3 constant_dynamic-update-slice_fusion.6
  257.3 1.0 constant_dynamic-update-slice_fusion.5
  258.3 1.1 constant_dynamic-update-slice_fusion.4
  259.4 2.3 constant_dynamic-update-slice_fusion.3
  261.6 2.3 constant_dynamic-update-slice_fusion.2
  263.9 0.0 copy-start.3
  263.9 1.1 constant_dynamic-update-slice_fusion.1
  265.0 1.1 constant_dynamic-update-slice_fusion
  266.1 0.0 all-gather.10.cloned.1.call-done
  266.1 3.1 fusion.1
  269.2 20.0 %all-gather.14.cloned.1.call-done = bf16[2048,1024]{1,0:T(8,128)(2,1)} async-done(((bf16[512,1024]{1,0:T(8,128)(2,1)}), bf16[2048,1024]{1,0:T(8,128)(2,1)}) %all-gather.14.cloned.1.call-update) | async-done | bytes 4194320 | tf_op jit(solution)/shard_map/all_gather | solution.py:52
  289.3 0.0 copy-done.3
  289.3 10.0 %fusion.4 = f32[8,128,1024]{2,1,0:T(8,128)} fusion(bf16[2048,1024]{1,0:T(8,128)(2,1)} %all-gather.14.cloned.1.call-done, bf16[8,2048,128]{1,2,0:T(8,128)(2,1)} %all-gather.10.cloned.1.call-done, f32[2048]{0:T(1024)S(1)} %copy-done.3, f32[8,128]{1,0:T(8,128)S(1)} %add_rsqrt_fusion), kind=kOutput, calls=%fused_computation.6 | convolution fusion | flops 4303355904 | bytes 12595200 | tf_op jit(solution)/shard_map/ukc,kf->ucf/dot_general | solution.py:49
  299.2 69.5 %all-gather.12.cloned.1.call-done = bf16[2048,1024]{1,0:T(8,128)(2,1)} async-done(((bf16[512,1024]{1,0:T(8,128)(2,1)}), bf16[2048,1024]{1,0:T(8,128)(2,1)}) %all-gather.12.cloned.1.call-update) | async-done | bytes 4194320 | tf_op jit(solution)/shard_map/all_gather | solution.py:46
  368.8 15.8 %fusion.11 = bf16[2048,8,128]{2,0,1:T(8,128)(2,1)} fusion(bf16[1024,4096]{0,1:T(8,128)(2,1)} %constant_dynamic-update-slice_fusion, s32[]{:T(128)S(6)} %select_n.21, f32[8,128,1024]{2,1,0:T(8,128)} %fusion.4, bf16[2048,1024]{1,0:T(8,128)(2,1)} %all-gather.12.cloned.1.call-done, bf16[8,2048,128]{1,2,0:T(8,128)(2,1)} %all-gather.10.cloned.1.call-done, ...), kind=kOutput, calls=%fused_computation.14 | convolution fusion | flops 8606711808 | bytes 20983812 | tf_op jit(solution)/shard_map/ucf,fk->kuc/dot_general | solution.py:72
  384.6 0.0 reduce-scatter.5.cloned.1.call-update
  384.6 49.7 %reduce-scatter.5.cloned.1.call-done = bf16[256,8,128]{2,0,1:T(8,128)(2,1)} async-done(((bf16[2048,8,128]{2,0,1:T(8,128)(2,1)}), bf16[256,8,128]{2,0,1:T(8,128)(2,1)}) %reduce-scatter.5.cloned.1.call-update) | async-done | bytes 524304 | tf_op jit(solution)/shard_map/reduce_scatter | solution.py:71
  (1 shorter events, 0.0 us)
Async XLA Ops:
  6.5 42.0 %copy-start = (bf16[256,2048]{1,0:T(8,128)(2,1)S(1)}, bf16[256,2048]{1,0:T(8,128)(2,1)}, u32[]{:S(2)}) copy-start(bf16[256,2048]{1,0:T(8,128)(2,1)} %param.11) | copy-start | bytes 3145732
  6.5 42.0 %all-gather.6.cloned.1.call-start = ((), (), s32[]{:S(2)}) async-start(), calls=%async_computation.2 | async-start | bytes 4718592 | tf_op jit(solution)/shard_map/all_gather | solution.py:22
  7.3 100.8 %reduce-scatter.3.cloned.1.call-start = ((), (), s32[]{:S(2)}) async-start(), calls=%async_computation.3 | async-start | bytes 4718592 | tf_op jit(solution)/shard_map/reduce_scatter | solution.py:31
  56.7 0.7 copy-start.2
  56.8 81.7 %all-gather.8.cloned.1.call-start = ((), (), s32[]{:S(2)}) async-start(), calls=%async_computation.4 | async-start | bytes 2359296 | tf_op jit(solution)/shard_map/all_gather | solution.py:33
  110.5 34.3 %copy-start.1 = (bf16[1024,512]{1,0:T(8,128)(2,1)S(1)}, bf16[1024,512]{1,0:T(8,128)(2,1)}, u32[]{:S(2)}) copy-start(bf16[1024,512]{1,0:T(8,128)(2,1)} %param.15) | copy-start | bytes 3145732
  110.5 155.6 %all-gather.10.cloned.1.call-start = ((), (), s32[]{:S(2)}) async-start(), calls=%async_computation.5 | async-start | bytes 4718592 | tf_op jit(solution)/shard_map/all_gather | solution.py:37
  143.6 145.6 %all-gather.14.cloned.1.call-start = ((), (), s32[]{:S(2)}) async-start(), calls=%async_computation.7 | async-start | bytes 5242880 | tf_op jit(solution)/shard_map/all_gather | solution.py:52
  144.2 224.6 %all-gather.12.cloned.1.call-start = ((), (), s32[]{:S(2)}) async-start(), calls=%async_computation.6 | async-start | bytes 5242880 | tf_op jit(solution)/shard_map/all_gather | solution.py:46
  144.8 289.6 %reduce-scatter.5.cloned.1.call-start = ((), (), s32[]{:S(2)}) async-start(), calls=%async_computation.8 | async-start | bytes 4718592 | tf_op jit(solution)/shard_map/reduce_scatter | solution.py:71
  145.4 27.1 %collective-permute-start = (bf16[1024,512]{0,1:T(8,128)(2,1)S(1)}, bf16[1024,512]{0,1:T(8,128)(2,1)S(1)}, u32[]{:S(2)}, u32[]{:S(2)}) collective-permute-start(bf16[1024,512]{0,1:T(8,128)(2,1)S(1)} %copy.9), channel_id=1, source_target_pairs={{0,8},{8,16},{16,24},{24,0},{1,9},{9,17},{17,25},{25,1},{2,10},{10... | collective-permute-start | bytes 3145736 | tf_op jit(solution)/shard_map/ppermute | solution.py:64
  172.5 31.4 %collective-permute-start.1 = (bf16[1024,512]{0,1:T(8,128)(2,1)S(1)}, bf16[1024,512]{0,1:T(8,128)(2,1)}, u32[]{:S(2)}, u32[]{:S(2)}) collective-permute-start(bf16[1024,512]{0,1:T(8,128)(2,1)S(1)} %collective-permute-done), channel_id=1, source_target_pairs={{0,8},{8,16},{16,24},{24,0},{1,9},{9,17},{17,25},{25,1},{2,10},{10... | collective-permute-start | bytes 3145736 | tf_op jit(solution)/shard_map/ppermute | solution.py:64
  203.9 48.8 %collective-permute-start.2 = (bf16[1024,512]{0,1:T(8,128)(2,1)}, bf16[1024,512]{0,1:T(8,128)(2,1)}, u32[]{:S(2)}, u32[]{:S(2)}) collective-permute-start(bf16[1024,512]{0,1:T(8,128)(2,1)} %collective-permute-done.1), channel_id=1, source_target_pairs={{0,8},{8,16},{16,24},{24,0},{1,9},{9,17},{17,25},{25,1},{2,10},{10... | collective-permute-start | bytes 3145736 | tf_op jit(solution)/shard_map/ppermute | solution.py:64
  263.9 25.3 %copy-start.3 = (f32[2048]{0:T(1024)S(1)}, f32[2048]{0:T(1024)}, u32[]{:S(2)}) copy-start(f32[2048]{0:T(1024)} %param.12) | copy-start | bytes 24580
Sparse Core Ops, SparseCore 0:
  9.2 39.2 all-gather.5
  56.9 51.0 reduce-scatter.2
  110.6 27.7 all-gather.7
  143.7 37.3 all-gather.9
  182.5 106.6 all-gather.13
  290.7 78.0 all-gather.11
  384.7 49.5 reduce-scatter.4
